TPU v7x, 32 devices: a whole 2x2x4 slice. The times are simulated.
32 devices in a mesh: blk: 8 (over y, x, core), batch: 4 (over z).
Axes of the slice: x: 2, y: 2, z: 4, core: 2. Of those that a mesh axis runs over, the one named last changes fastest.
Arguments:
- query_base: bfloat16 [32, 36864], P(('batch', 'blk')), may hold values from -14 to 14
- query_latent: bfloat16 [32, 1536], P(('batch', 'blk')), may hold values from -6 to 6
- tenant_ids: int32 [32], P('batch'), may hold values from 0 to 3
- adapter_qa: bfloat16 [4, 1536, 16], replicated, may hold values from -0.15625 to 0.15625
- adapter_qb: bfloat16 [4, 16, 36864], replicated, may hold values from -0.29882812 to 0.29882812
- prefix_cache: bfloat16 [32768, 576], P('blk'), may hold values from -6 to 6
- prefix_mask: int32 [32, 256], P('batch', 'blk'), may hold values 0 or 1
- suffix_cache: bfloat16 [32, 4096, 576], P(('batch', 'blk')), may hold values from -6 to 6
- suffix_blocks: int32 [8, 4], P('blk'), may hold values from 1 to 32, 40 in all within a row
- new_latent: bfloat16 [32, 576], P(('batch', 'blk')), may hold values from -6 to 6
- value_up: bfloat16 [64, 512, 128], P('blk'), may hold values from -0.25 to 0.25
- out_weight: bfloat16 [8192, 7168], P('blk'), may hold values from -0.0625 to 0.0625
- adapter_oa: bfloat16 [4, 8192, 16], P(None, 'blk'), may hold values from -0.0625 to 0.0625
- adapter_ob: bfloat16 [4, 16, 7168], replicated, may hold values from -1.5 to 1.5
Outputs:
- attention_out: bfloat16 [32, 7168], P(('batch', 'blk'))
Inputs may be any that keep to these rules, and one draw needn't show every extreme that they name: `suffix_blocks`: each row holds 40 blocks in all, and its largest entry is exactly 32.
All inputs are finite; a program needn't handle non-finite values. No bound on the sum of `prefix_mask` on one device may be relied on, other than what follows from the above.
Results may differ from a plain program's by a relative error of at most 0.025.
Values may be sent and summed in bfloat16 or wider, within the bound.
A program may use at most 128 MiB of HBM per device.

v0:
```python
import jax
import jax.numpy as jnp
from jax import lax
from jax.sharding import PartitionSpec as P

D = 7168
H = 64
LAT = 512
QK = 192
RANK = 16
BLOCK = 128
KV = 576
floor_score = -1e30


def passed_along(block, axis, distance):
    devices = range(lax.axis_size(axis))
    route = [((i - distance) % len(devices), i) for i in devices]
    return lax.ppermute(block, axis, route)


def combine_parts(first_part, second_part):
    peak = jnp.maximum(first_part[0], second_part[0])
    first_scale = jnp.exp(first_part[0] - peak)
    second_scale = jnp.exp(second_part[0] - peak)
    totals = first_part[1] * first_scale + second_part[1] * second_scale
    sums = first_part[2] * first_scale[..., None] + second_part[2] * second_scale[..., None]
    return (peak, totals, sums)


def partial_softmax(scores, live_keys, values, per_row):
    masked = jnp.where(live_keys, scores, -jnp.inf)
    peak = jnp.maximum(jnp.max(masked, axis=-1), floor_score)
    weights = jnp.exp(masked - peak[..., None])
    totals = jnp.sum(weights, axis=-1)
    weights_low = weights.astype(jnp.bfloat16)
    if per_row:
        sums = jnp.einsum("nht,ntl->nhl", weights_low, values, preferred_element_type=jnp.float32)
    else:
        sums = jnp.einsum("nht,tl->nhl", weights_low, values, preferred_element_type=jnp.float32)
    return (peak, totals, sums)


def prefix_part(queries, mask_rows, prefix_cache, score_scale):
    count_rows = queries.shape[0]
    blocks_here = mask_rows.shape[1]
    scores = (
        jnp.einsum("nhk,tk->nht", queries, prefix_cache, preferred_element_type=jnp.float32)
        * score_scale
    )
    live_keys = jnp.broadcast_to((mask_rows > 0)[:, :, None], (count_rows, blocks_here, BLOCK))
    live_keys = live_keys.reshape(count_rows, 1, blocks_here * BLOCK)
    return partial_softmax(scores, live_keys, prefix_cache[:, :LAT], False)


def empty_parts(count_rows):
    return (
        jnp.full((count_rows, H), floor_score, jnp.float32),
        jnp.zeros((count_rows, H), jnp.float32),
        jnp.zeros((count_rows, H, LAT), jnp.float32),
    )


def on_device(
    query_base,
    query_latent,
    tenant_ids,
    adapter_qa,
    adapter_qb,
    prefix_cache,
    prefix_mask,
    suffix_cache,
    suffix_blocks,
    new_latent,
    value_up,
    out_weight,
    adapter_oa,
    adapter_ob,
):
    score_scale = QK ** (-0.5)
    blk_count = lax.axis_size("blk")
    blk_index = lax.axis_index("blk")
    batch_index = lax.axis_index("batch")
    owned_rows = query_base.shape[0]
    group_rows = owned_rows * blk_count
    tenants = adapter_qa.shape[0]
    own_tenant = lax.dynamic_slice_in_dim(tenant_ids, blk_index * owned_rows, owned_rows)
    tenant_hit = (own_tenant[:, None] == jnp.arange(tenants)[None, :]).astype(jnp.float32)
    low_every = jnp.einsum(
        "rq,tqk->rtk", query_latent, adapter_qa, preferred_element_type=jnp.float32
    )
    low_query = jnp.sum(low_every * tenant_hit[:, :, None], axis=1).astype(jnp.bfloat16)
    low_spread = (tenant_hit.astype(jnp.bfloat16)[:, :, None] * low_query[:, None, :]).reshape(
        owned_rows, tenants * RANK
    )
    delta_query = jnp.dot(
        low_spread, adapter_qb.reshape(tenants * RANK, H * KV), preferred_element_type=jnp.float32
    )
    query = (query_base.astype(jnp.float32) + delta_query).astype(jnp.bfloat16)
    query_heads = query.reshape(owned_rows, H, KV)

    def travel_step(visit_step, state):
        moving, running = state
        anchor = (blk_index - visit_step) % blk_count
        mask_rows = lax.dynamic_slice_in_dim(prefix_mask, anchor * owned_rows, owned_rows)
        fresh_part = prefix_part(
            moving.reshape(owned_rows, H, KV), mask_rows, prefix_cache, score_scale
        )
        running = combine_parts(running, fresh_part)
        moving = passed_along(moving, "blk", 1)
        running = passed_along((running[0], running[1], running[2]), "blk", 1)
        return (moving, running)

    final_state = lax.fori_loop(0, blk_count, travel_step, (query, empty_parts(owned_rows)))
    prefix_result = final_state[1]
    length_row = suffix_blocks[0]
    own_lengths = lax.dynamic_slice_in_dim(length_row, batch_index * owned_rows, owned_rows)
    slot_count = suffix_cache.shape[1]
    scores = (
        jnp.einsum("nhk,ntk->nht", query_heads, suffix_cache, preferred_element_type=jnp.float32)
        * score_scale
    )
    live_keys = jnp.arange(slot_count)[None, None, :] < (own_lengths * BLOCK)[:, None, None]
    suffix_result = partial_softmax(scores, live_keys, suffix_cache[:, :, :LAT], True)
    new_scores = (
        jnp.einsum("nhk,nk->nh", query_heads, new_latent, preferred_element_type=jnp.float32)
        * score_scale
    )
    new_values = jnp.broadcast_to(
        new_latent[:, None, :LAT].astype(jnp.float32), (owned_rows, H, LAT)
    )
    new_part = (new_scores, jnp.ones_like(new_scores), new_values)
    combined = combine_parts(combine_parts(prefix_result, suffix_result), new_part)
    context = (combined[2] / combined[1][..., None]).astype(jnp.bfloat16)
    head_rows = lax.all_to_all(context, "blk", split_axis=1, concat_axis=0, tiled=True)
    head_out = jnp.einsum("rhl,hlv->rhv", head_rows, value_up, preferred_element_type=jnp.float32)
    head_out = head_out.astype(jnp.bfloat16).reshape(group_rows, -1)
    group_hit = (tenant_ids[:, None] == jnp.arange(tenants)[None, :]).astype(jnp.float32)
    adapter_up = adapter_ob.reshape(tenants * RANK, D).astype(jnp.float32)
    projected = jnp.dot(head_out, out_weight, preferred_element_type=jnp.float32)
    low_every_out = jnp.einsum(
        "rk,tkj->rtj", head_out, adapter_oa, preferred_element_type=jnp.float32
    )
    low_spread_out = (low_every_out * group_hit[:, :, None]).reshape(
        lax.axis_size("blk") * owned_rows, tenants * RANK
    )
    return lax.psum_scatter(
        (projected + jnp.dot(low_spread_out, adapter_up, precision=lax.Precision.HIGHEST)).astype(
            jnp.bfloat16
        ),
        "blk",
        scatter_dimension=0,
        tiled=True,
    )


def solution(mesh):
    placed = (
        P(("batch", "blk"), None),
        P(("batch", "blk"), None),
        P("batch"),
        P(),
        P(),
        P("blk", None),
        P("batch", "blk"),
        P(("batch", "blk"), None, None),
        P("blk", None),
        P(("batch", "blk"), None),
        P("blk", None, None),
        P("blk", None),
        P(None, "blk", None),
        P(),
    )
    return jax.shard_map(
        on_device, mesh=mesh, in_specs=placed, out_specs=P(("batch", "blk"), None), check_vma=False
    )
```

profile of v0, /device:TPU:0, one launch (start us, length us, event | category | flops | bytes accessed | tf_op | source)
XLA Modules:
  0.0 224.7 jit_solution(18082579267390969847)
XLA Ops:
  12.9 3.2 %fusion.80 = (bf16[36864]{0:T(1024)(128)(2,1)S(1)}, bf16[1,36864]{1,0:T(2,128)(2,1)S(1)}) fusion(bf16[64,1]{0,1:T(2,128)(2,1)S(1)} %reshape.366, bf16[64,36864]{1,0:T(8,128)(2,1)} %bitcast.182, bf16[1,36864]{1,0:T(2,128)(2,1)} %param.16), kind=kOutput, calls=%fused_computation.86 | convolution fusion | flops 4829184 | bytes 4939904 | tf_op jit(solution)/shard_map/dot_general | solution.py:96
  16.2 3.5 %fusion.82 = (f32[64]{0:T(128)S(1)}, f32[64,4096]{1,0:T(8,128)S(1)}) fusion(bf16[64,576]{1,0:T(8,128)(2,1)S(1)} %reshape.358, bf16[1,4096,576]{1,2,0:T(8,128)(2,1)} %param.23, pred[4096]{0:T(1024)(128)(4,1)S(1)} %iota_compare_fusion), kind=kOutput, calls=%fused_computation.88 | convolution fusion | flops 302776256 | bytes 5845248 | tf_op jit(solution)/shard_map/nhk,ntk->nht/dot_general | solution.py:120
  20.7 119.1 %while.21 = (s32[]{:T(128)}, bf16[1,36864]{1,0:T(2,128)(2,1)S(1)}, f32[1,64]{1,0:T(1,128)S(1)}, f32[1,64]{1,0:T(1,128)S(1)}, f32[1,64,512]{2,1,0:T(8,128)}, /*in...) while((s32[]{:T(128)}, bf16[1,36864]{1,0:T(2,128)(2,1)S(1)}, ...), condition=%wide.region_4.5_spmd, body=%wide.region_1.4_spmd.sunk | while | flops 572359104 | bytes 32546200 | solution.py:114
  22.2 3.6 %fusion.109 = (f32[64]{0:T(128)S(1)}, f32[64,4096]{1,0:T(8,128)S(1)}) fusion(bf16[64,576]{1,0:T(8,128)(2,1)S(1)} %reshape.381, bf16[4096,576]{0,1:T(8,128)(2,1)} %get-tuple-element.336, pred[4096]{0:T(1024)(128)(4,1)S(1)} %broadcast_bitcast_fusion.2), kind=kOutput, calls=%fused_computation.85.clone.1 | convolution fusion | flops 302776256 | bytes 5845248 | tf_op jit(solution)/shard_map/while/body/eval_jaxpr/nhk,tk->nht/dot_general | solution.py:48
  29.0 2.6 %collective-permute-start = (bf16[1,36864]{1,0:T(2,128)(2,1)S(1)}, bf16[1,36864]{1,0:T(2,128)(2,1)S(1)}, u32[]{:S(2)}, u32[]{:S(2)}) collective-permute-start(bf16[1,36864]{1,0:T(2,128)(2,1)S(1)} %copy.35), channel_id=1, source_target_pairs={{28,0},{0,4},{4,8},{8,12},{12,16},{16,20},{20,24},{24,28},{29,1},{... | collective-permute-start | bytes 221192 | tf_op jit(solution)/shard_map/while/body/eval_jaxpr/ppermute | solution.py:19
  33.2 3.0 %collective-permute-done.1 = f32[1,64]{1,0:T(1,128)S(1)} collective-permute-done((f32[1,64]{1,0:T(1,128)S(1)}, f32[1,64]{1,0:T(1,128)S(1)}, u32[]{:S(2)}, u32[]{:S(2)}) %collective-permute-start.1) | collective-permute-done | bytes 288 | tf_op jit(solution)/shard_map/while/body/eval_jaxpr/ppermute | solution.py:19
  37.7 3.6 %fusion.109 = (f32[64]{0:T(128)S(1)}, f32[64,4096]{1,0:T(8,128)S(1)}) fusion(bf16[64,576]{1,0:T(8,128)(2,1)S(1)} %reshape.381, bf16[4096,576]{0,1:T(8,128)(2,1)} %get-tuple-element.336, pred[4096]{0:T(1024)(128)(4,1)S(1)} %broadcast_bitcast_fusion.2), kind=kOutput, calls=%fused_computation.85.clone.1 | convolution fusion | flops 302776256 | bytes 5845248 | tf_op jit(solution)/shard_map/while/body/eval_jaxpr/nhk,tk->nht/dot_general | solution.py:48
  45.6 2.4 %collective-permute-start.2 = (f32[1,64]{1,0:T(1,128)S(1)}, f32[1,64]{1,0:T(1,128)S(1)}, u32[]{:S(2)}, u32[]{:S(2)}) collective-permute-start(f32[1,64]{1,0:T(1,128)S(1)} %get-tuple-element.300), channel_id=1, source_target_pairs={{28,0},{0,4},{4,8},{8,12},{12,16},{16,20},{20,24},{24,28},{29,1},{... | collective-permute-start | bytes 776 | tf_op jit(solution)/shard_map/while/body/eval_jaxpr/ppermute | solution.py:19
  48.0 3.0 %collective-permute-done.1 = f32[1,64]{1,0:T(1,128)S(1)} collective-permute-done((f32[1,64]{1,0:T(1,128)S(1)}, f32[1,64]{1,0:T(1,128)S(1)}, u32[]{:S(2)}, u32[]{:S(2)}) %collective-permute-start.1) | collective-permute-done | bytes 288 | tf_op jit(solution)/shard_map/while/body/eval_jaxpr/ppermute | solution.py:19
  52.5 3.6 %fusion.109 = (f32[64]{0:T(128)S(1)}, f32[64,4096]{1,0:T(8,128)S(1)}) fusion(bf16[64,576]{1,0:T(8,128)(2,1)S(1)} %reshape.381, bf16[4096,576]{0,1:T(8,128)(2,1)} %get-tuple-element.336, pred[4096]{0:T(1024)(128)(4,1)S(1)} %broadcast_bitcast_fusion.2), kind=kOutput, calls=%fused_computation.85.clone.1 | convolution fusion | flops 302776256 | bytes 5845248 | tf_op jit(solution)/shard_map/while/body/eval_jaxpr/nhk,tk->nht/dot_general | solution.py:48
  59.5 3.3 %collective-permute-start.2 = (f32[1,64]{1,0:T(1,128)S(1)}, f32[1,64]{1,0:T(1,128)S(1)}, u32[]{:S(2)}, u32[]{:S(2)}) collective-permute-start(f32[1,64]{1,0:T(1,128)S(1)} %get-tuple-element.300), channel_id=1, source_target_pairs={{28,0},{0,4},{4,8},{8,12},{12,16},{16,20},{20,24},{24,28},{29,1},{... | collective-permute-start | bytes 776 | tf_op jit(solution)/shard_map/while/body/eval_jaxpr/ppermute | solution.py:19
  62.8 3.0 %collective-permute-done.1 = f32[1,64]{1,0:T(1,128)S(1)} collective-permute-done((f32[1,64]{1,0:T(1,128)S(1)}, f32[1,64]{1,0:T(1,128)S(1)}, u32[]{:S(2)}, u32[]{:S(2)}) %collective-permute-start.1) | collective-permute-done | bytes 288 | tf_op jit(solution)/shard_map/while/body/eval_jaxpr/ppermute | solution.py:19
  67.3 3.6 %fusion.109 = (f32[64]{0:T(128)S(1)}, f32[64,4096]{1,0:T(8,128)S(1)}) fusion(bf16[64,576]{1,0:T(8,128)(2,1)S(1)} %reshape.381, bf16[4096,576]{0,1:T(8,128)(2,1)} %get-tuple-element.336, pred[4096]{0:T(1024)(128)(4,1)S(1)} %broadcast_bitcast_fusion.2), kind=kOutput, calls=%fused_computation.85.clone.1 | convolution fusion | flops 302776256 | bytes 5845248 | tf_op jit(solution)/shard_map/while/body/eval_jaxpr/nhk,tk->nht/dot_general | solution.py:48
  74.2 3.4 %collective-permute-start.2 = (f32[1,64]{1,0:T(1,128)S(1)}, f32[1,64]{1,0:T(1,128)S(1)}, u32[]{:S(2)}, u32[]{:S(2)}) collective-permute-start(f32[1,64]{1,0:T(1,128)S(1)} %get-tuple-element.300), channel_id=1, source_target_pairs={{28,0},{0,4},{4,8},{8,12},{12,16},{16,20},{20,24},{24,28},{29,1},{... | collective-permute-start | bytes 776 | tf_op jit(solution)/shard_map/while/body/eval_jaxpr/ppermute | solution.py:19
  77.6 3.0 %collective-permute-done.1 = f32[1,64]{1,0:T(1,128)S(1)} collective-permute-done((f32[1,64]{1,0:T(1,128)S(1)}, f32[1,64]{1,0:T(1,128)S(1)}, u32[]{:S(2)}, u32[]{:S(2)}) %collective-permute-start.1) | collective-permute-done | bytes 288 | tf_op jit(solution)/shard_map/while/body/eval_jaxpr/ppermute | solution.py:19
  82.1 3.6 %fusion.109 = (f32[64]{0:T(128)S(1)}, f32[64,4096]{1,0:T(8,128)S(1)}) fusion(bf16[64,576]{1,0:T(8,128)(2,1)S(1)} %reshape.381, bf16[4096,576]{0,1:T(8,128)(2,1)} %get-tuple-element.336, pred[4096]{0:T(1024)(128)(4,1)S(1)} %broadcast_bitcast_fusion.2), kind=kOutput, calls=%fused_computation.85.clone.1 | convolution fusion | flops 302776256 | bytes 5845248 | tf_op jit(solution)/shard_map/while/body/eval_jaxpr/nhk,tk->nht/dot_general | solution.py:48
  89.0 3.4 %collective-permute-start.2 = (f32[1,64]{1,0:T(1,128)S(1)}, f32[1,64]{1,0:T(1,128)S(1)}, u32[]{:S(2)}, u32[]{:S(2)}) collective-permute-start(f32[1,64]{1,0:T(1,128)S(1)} %get-tuple-element.300), channel_id=1, source_target_pairs={{28,0},{0,4},{4,8},{8,12},{12,16},{16,20},{20,24},{24,28},{29,1},{... | collective-permute-start | bytes 776 | tf_op jit(solution)/shard_map/while/body/eval_jaxpr/ppermute | solution.py:19
  92.4 3.0 %collective-permute-done.1 = f32[1,64]{1,0:T(1,128)S(1)} collective-permute-done((f32[1,64]{1,0:T(1,128)S(1)}, f32[1,64]{1,0:T(1,128)S(1)}, u32[]{:S(2)}, u32[]{:S(2)}) %collective-permute-start.1) | collective-permute-done | bytes 288 | tf_op jit(solution)/shard_map/while/body/eval_jaxpr/ppermute | solution.py:19
  96.9 3.6 %fusion.109 = (f32[64]{0:T(128)S(1)}, f32[64,4096]{1,0:T(8,128)S(1)}) fusion(bf16[64,576]{1,0:T(8,128)(2,1)S(1)} %reshape.381, bf16[4096,576]{0,1:T(8,128)(2,1)} %get-tuple-element.336, pred[4096]{0:T(1024)(128)(4,1)S(1)} %broadcast_bitcast_fusion.2), kind=kOutput, calls=%fused_computation.85.clone.1 | convolution fusion | flops 302776256 | bytes 5845248 | tf_op jit(solution)/shard_map/while/body/eval_jaxpr/nhk,tk->nht/dot_general | solution.py:48
  103.8 3.4 %collective-permute-start.2 = (f32[1,64]{1,0:T(1,128)S(1)}, f32[1,64]{1,0:T(1,128)S(1)}, u32[]{:S(2)}, u32[]{:S(2)}) collective-permute-start(f32[1,64]{1,0:T(1,128)S(1)} %get-tuple-element.300), channel_id=1, source_target_pairs={{28,0},{0,4},{4,8},{8,12},{12,16},{16,20},{20,24},{24,28},{29,1},{... | collective-permute-start | bytes 776 | tf_op jit(solution)/shard_map/while/body/eval_jaxpr/ppermute | solution.py:19
  107.2 3.0 %collective-permute-done.1 = f32[1,64]{1,0:T(1,128)S(1)} collective-permute-done((f32[1,64]{1,0:T(1,128)S(1)}, f32[1,64]{1,0:T(1,128)S(1)}, u32[]{:S(2)}, u32[]{:S(2)}) %collective-permute-start.1) | collective-permute-done | bytes 288 | tf_op jit(solution)/shard_map/while/body/eval_jaxpr/ppermute | solution.py:19
  111.7 3.6 %fusion.109 = (f32[64]{0:T(128)S(1)}, f32[64,4096]{1,0:T(8,128)S(1)}) fusion(bf16[64,576]{1,0:T(8,128)(2,1)S(1)} %reshape.381, bf16[4096,576]{0,1:T(8,128)(2,1)} %get-tuple-element.336, pred[4096]{0:T(1024)(128)(4,1)S(1)} %broadcast_bitcast_fusion.2), kind=kOutput, calls=%fused_computation.85.clone.1 | convolution fusion | flops 302776256 | bytes 5845248 | tf_op jit(solution)/shard_map/while/body/eval_jaxpr/nhk,tk->nht/dot_general | solution.py:48
  118.6 3.4 %collective-permute-start.2 = (f32[1,64]{1,0:T(1,128)S(1)}, f32[1,64]{1,0:T(1,128)S(1)}, u32[]{:S(2)}, u32[]{:S(2)}) collective-permute-start(f32[1,64]{1,0:T(1,128)S(1)} %get-tuple-element.300), channel_id=1, source_target_pairs={{28,0},{0,4},{4,8},{8,12},{12,16},{16,20},{20,24},{24,28},{29,1},{... | collective-permute-start | bytes 776 | tf_op jit(solution)/shard_map/while/body/eval_jaxpr/ppermute | solution.py:19
  122.0 3.0 %collective-permute-done.1 = f32[1,64]{1,0:T(1,128)S(1)} collective-permute-done((f32[1,64]{1,0:T(1,128)S(1)}, f32[1,64]{1,0:T(1,128)S(1)}, u32[]{:S(2)}, u32[]{:S(2)}) %collective-permute-start.1) | collective-permute-done | bytes 288 | tf_op jit(solution)/shard_map/while/body/eval_jaxpr/ppermute | solution.py:19
  126.5 3.6 %fusion.109 = (f32[64]{0:T(128)S(1)}, f32[64,4096]{1,0:T(8,128)S(1)}) fusion(bf16[64,576]{1,0:T(8,128)(2,1)S(1)} %reshape.381, bf16[4096,576]{0,1:T(8,128)(2,1)} %get-tuple-element.336, pred[4096]{0:T(1024)(128)(4,1)S(1)} %broadcast_bitcast_fusion.2), kind=kOutput, calls=%fused_computation.85.clone.1 | convolution fusion | flops 302776256 | bytes 5845248 | tf_op jit(solution)/shard_map/while/body/eval_jaxpr/nhk,tk->nht/dot_general | solution.py:48
  133.4 3.4 %collective-permute-start.2 = (f32[1,64]{1,0:T(1,128)S(1)}, f32[1,64]{1,0:T(1,128)S(1)}, u32[]{:S(2)}, u32[]{:S(2)}) collective-permute-start(f32[1,64]{1,0:T(1,128)S(1)} %get-tuple-element.300), channel_id=1, source_target_pairs={{28,0},{0,4},{4,8},{8,12},{12,16},{16,20},{20,24},{24,28},{29,1},{... | collective-permute-start | bytes 776 | tf_op jit(solution)/shard_map/while/body/eval_jaxpr/ppermute | solution.py:19
  136.8 3.0 %collective-permute-done.1 = f32[1,64]{1,0:T(1,128)S(1)} collective-permute-done((f32[1,64]{1,0:T(1,128)S(1)}, f32[1,64]{1,0:T(1,128)S(1)}, u32[]{:S(2)}, u32[]{:S(2)}) %collective-permute-start.1) | collective-permute-done | bytes 288 | tf_op jit(solution)/shard_map/while/body/eval_jaxpr/ppermute | solution.py:19
  140.0 3.8 %fusion.53 = bf16[1,64,512]{2,1,0:T(8,128)(2,1)S(1)} fusion(bf16[1,4096,576]{1,2,0:T(8,128)(2,1)} %param.23, f32[64,4096]{1,0:T(8,128)S(1)} %get-tuple-element.239, f32[64]{0:T(128)S(1)} %broadcast_maximum_fusion.1, f32[1,64,512]{2,1,0:T(8,128)} %get-tuple-element.206, f32[64]{0:T(128)S(1)} %get-tuple-element.232, f32[64]{0:T(128)S(1)} %get-tuple-element.233, ...), kind=kOutput, calls=%fused_computation.45 | convolution fusion | flops 269221888 | bytes 5443072 | tf_op jit(solution)/shard_map/nht,ntl->nhl/dot_general | solution.py:38
  146.1 3.5 %all-to-all-start = ((bf16[8,2,2048]{2,1,0:T(2,128)(2,1)}), bf16[8,2,2048]{2,1,0:T(2,128)(2,1)S(1)}, u32[]{:S(2)}, u32[]{:S(2)}) async-start(bf16[8,2,2048]{2,1,0:T(2,128)(2,1)} %reshape.378), calls=%async_computation | async-start | bytes 131072 | tf_op jit(solution)/shard_map/all_to_all | solution.py:135
  149.7 5.0 %all-to-all-done = bf16[8,2,2048]{2,1,0:T(2,128)(2,1)S(1)} async-done(((bf16[8,2,2048]{2,1,0:T(2,128)(2,1)}), bf16[8,2,2048]{2,1,0:T(2,128)(2,1)S(1)}, u32[]{:S(2)}, u32[]{:S(2)}) %all-to-all-start) | async-done | bytes 65568 | tf_op jit(solution)/shard_map/all_to_all | solution.py:135
  156.3 7.8 %fusion.21 = bf16[8,7168]{1,0:T(8,128)(2,1)} fusion(f32[8,7168]{1,0:T(8,128)S(1)} %convolution_bitcast_fusion, bf16[1024,7168]{1,0:T(8,128)(2,1)} %param.27, bf16[8,8,128]{2,1,0:T(8,128)(2,1)S(1)} %convolution_convert_fusion), kind=kOutput, calls=%fused_computation.26 | convolution fusion | flops 117555200 | bytes 15040512 | tf_op jit(solution)/shard_map/dot_general | solution.py:140
  164.8 50.9 %all-reduce.3.cloned.1.call-done = bf16[8,7168]{1,0:T(8,128)(2,1)} async-done(((bf16[8,7168]{1,0:T(8,128)(2,1)}), bf16[8,7168]{1,0:T(8,128)(2,1)}) %all-reduce.3.cloned.1.call-update) | async-done | bytes 114704
  (178 shorter events, 54.7 us)
Async XLA Ops:
  28.5 7.7 %collective-permute-start.3 = (f32[1,64,512]{2,1,0:T(8,128)S(1)}, f32[1,64,512]{2,1,0:T(8,128)}, u32[]{:S(2)}, u32[]{:S(2)}) collective-permute-start(f32[1,64,512]{2,1,0:T(8,128)S(1)} %fusion.112), channel_id=1, source_target_pairs={{28,0},{0,4},{4,8},{8,12},{12,16},{16,20},{20,24},{24,28},{29,1},{... | collective-permute-start | bytes 393224 | tf_op jit(solution)/shard_map/while/body/eval_jaxpr/ppermute | solution.py:19
  29.0 7.2 %collective-permute-start = (bf16[1,36864]{1,0:T(2,128)(2,1)S(1)}, bf16[1,36864]{1,0:T(2,128)(2,1)S(1)}, u32[]{:S(2)}, u32[]{:S(2)}) collective-permute-start(bf16[1,36864]{1,0:T(2,128)(2,1)S(1)} %copy.35), channel_id=1, source_target_pairs={{28,0},{0,4},{4,8},{8,12},{12,16},{16,20},{20,24},{24,28},{29,1},{... | collective-permute-start | bytes 221192 | tf_op jit(solution)/shard_map/while/body/eval_jaxpr/ppermute | solution.py:19
  44.0 7.0 %collective-permute-start.3 = (f32[1,64,512]{2,1,0:T(8,128)S(1)}, f32[1,64,512]{2,1,0:T(8,128)}, u32[]{:S(2)}, u32[]{:S(2)}) collective-permute-start(f32[1,64,512]{2,1,0:T(8,128)S(1)} %fusion.112), channel_id=1, source_target_pairs={{28,0},{0,4},{4,8},{8,12},{12,16},{16,20},{20,24},{24,28},{29,1},{... | collective-permute-start | bytes 393224 | tf_op jit(solution)/shard_map/while/body/eval_jaxpr/ppermute | solution.py:19
  44.1 6.9 %collective-permute-start = (bf16[1,36864]{1,0:T(2,128)(2,1)S(1)}, bf16[1,36864]{1,0:T(2,128)(2,1)S(1)}, u32[]{:S(2)}, u32[]{:S(2)}) collective-permute-start(bf16[1,36864]{1,0:T(2,128)(2,1)S(1)} %copy.35), channel_id=1, source_target_pairs={{28,0},{0,4},{4,8},{8,12},{12,16},{16,20},{20,24},{24,28},{29,1},{... | collective-permute-start | bytes 221192 | tf_op jit(solution)/shard_map/while/body/eval_jaxpr/ppermute | solution.py:19
  45.5 5.5 %collective-permute-start.1 = (f32[1,64]{1,0:T(1,128)S(1)}, f32[1,64]{1,0:T(1,128)S(1)}, u32[]{:S(2)}, u32[]{:S(2)}) collective-permute-start(f32[1,64]{1,0:T(1,128)S(1)} %get-tuple-element.299), channel_id=1, source_target_pairs={{28,0},{0,4},{4,8},{8,12},{12,16},{16,20},{20,24},{24,28},{29,1},{... | collective-permute-start | bytes 776 | tf_op jit(solution)/shard_map/while/body/eval_jaxpr/ppermute | solution.py:19
  45.6 5.4 %collective-permute-start.2 = (f32[1,64]{1,0:T(1,128)S(1)}, f32[1,64]{1,0:T(1,128)S(1)}, u32[]{:S(2)}, u32[]{:S(2)}) collective-permute-start(f32[1,64]{1,0:T(1,128)S(1)} %get-tuple-element.300), channel_id=1, source_target_pairs={{28,0},{0,4},{4,8},{8,12},{12,16},{16,20},{20,24},{24,28},{29,1},{... | collective-permute-start | bytes 776 | tf_op jit(solution)/shard_map/while/body/eval_jaxpr/ppermute | solution.py:19
  58.8 7.0 %collective-permute-start.3 = (f32[1,64,512]{2,1,0:T(8,128)S(1)}, f32[1,64,512]{2,1,0:T(8,128)}, u32[]{:S(2)}, u32[]{:S(2)}) collective-permute-start(f32[1,64,512]{2,1,0:T(8,128)S(1)} %fusion.112), channel_id=1, source_target_pairs={{28,0},{0,4},{4,8},{8,12},{12,16},{16,20},{20,24},{24,28},{29,1},{... | collective-permute-start | bytes 393224 | tf_op jit(solution)/shard_map/while/body/eval_jaxpr/ppermute | solution.py:19
  58.9 6.9 %collective-permute-start = (bf16[1,36864]{1,0:T(2,128)(2,1)S(1)}, bf16[1,36864]{1,0:T(2,128)(2,1)S(1)}, u32[]{:S(2)}, u32[]{:S(2)}) collective-permute-start(bf16[1,36864]{1,0:T(2,128)(2,1)S(1)} %copy.35), channel_id=1, source_target_pairs={{28,0},{0,4},{4,8},{8,12},{12,16},{16,20},{20,24},{24,28},{29,1},{... | collective-permute-start | bytes 221192 | tf_op jit(solution)/shard_map/while/body/eval_jaxpr/ppermute | solution.py:19
  59.4 6.4 %collective-permute-start.1 = (f32[1,64]{1,0:T(1,128)S(1)}, f32[1,64]{1,0:T(1,128)S(1)}, u32[]{:S(2)}, u32[]{:S(2)}) collective-permute-start(f32[1,64]{1,0:T(1,128)S(1)} %get-tuple-element.299), channel_id=1, source_target_pairs={{28,0},{0,4},{4,8},{8,12},{12,16},{16,20},{20,24},{24,28},{29,1},{... | collective-permute-start | bytes 776 | tf_op jit(solution)/shard_map/while/body/eval_jaxpr/ppermute | solution.py:19
  59.5 6.3 %collective-permute-start.2 = (f32[1,64]{1,0:T(1,128)S(1)}, f32[1,64]{1,0:T(1,128)S(1)}, u32[]{:S(2)}, u32[]{:S(2)}) collective-permute-start(f32[1,64]{1,0:T(1,128)S(1)} %get-tuple-element.300), channel_id=1, source_target_pairs={{28,0},{0,4},{4,8},{8,12},{12,16},{16,20},{20,24},{24,28},{29,1},{... | collective-permute-start | bytes 776 | tf_op jit(solution)/shard_map/while/body/eval_jaxpr/ppermute | solution.py:19
  73.6 7.0 %collective-permute-start.3 = (f32[1,64,512]{2,1,0:T(8,128)S(1)}, f32[1,64,512]{2,1,0:T(8,128)}, u32[]{:S(2)}, u32[]{:S(2)}) collective-permute-start(f32[1,64,512]{2,1,0:T(8,128)S(1)} %fusion.112), channel_id=1, source_target_pairs={{28,0},{0,4},{4,8},{8,12},{12,16},{16,20},{20,24},{24,28},{29,1},{... | collective-permute-start | bytes 393224 | tf_op jit(solution)/shard_map/while/body/eval_jaxpr/ppermute | solution.py:19
  73.7 6.9 %collective-permute-start = (bf16[1,36864]{1,0:T(2,128)(2,1)S(1)}, bf16[1,36864]{1,0:T(2,128)(2,1)S(1)}, u32[]{:S(2)}, u32[]{:S(2)}) collective-permute-start(bf16[1,36864]{1,0:T(2,128)(2,1)S(1)} %copy.35), channel_id=1, source_target_pairs={{28,0},{0,4},{4,8},{8,12},{12,16},{16,20},{20,24},{24,28},{29,1},{... | collective-permute-start | bytes 221192 | tf_op jit(solution)/shard_map/while/body/eval_jaxpr/ppermute | solution.py:19
  73.7 6.8 %collective-permute-start.1 = (f32[1,64]{1,0:T(1,128)S(1)}, f32[1,64]{1,0:T(1,128)S(1)}, u32[]{:S(2)}, u32[]{:S(2)}) collective-permute-start(f32[1,64]{1,0:T(1,128)S(1)} %get-tuple-element.299), channel_id=1, source_target_pairs={{28,0},{0,4},{4,8},{8,12},{12,16},{16,20},{20,24},{24,28},{29,1},{... | collective-permute-start | bytes 776 | tf_op jit(solution)/shard_map/while/body/eval_jaxpr/ppermute | solution.py:19
  74.2 6.4 %collective-permute-start.2 = (f32[1,64]{1,0:T(1,128)S(1)}, f32[1,64]{1,0:T(1,128)S(1)}, u32[]{:S(2)}, u32[]{:S(2)}) collective-permute-start(f32[1,64]{1,0:T(1,128)S(1)} %get-tuple-element.300), channel_id=1, source_target_pairs={{28,0},{0,4},{4,8},{8,12},{12,16},{16,20},{20,24},{24,28},{29,1},{... | collective-permute-start | bytes 776 | tf_op jit(solution)/shard_map/while/body/eval_jaxpr/ppermute | solution.py:19
  88.4 7.0 %collective-permute-start.3 = (f32[1,64,512]{2,1,0:T(8,128)S(1)}, f32[1,64,512]{2,1,0:T(8,128)}, u32[]{:S(2)}, u32[]{:S(2)}) collective-permute-start(f32[1,64,512]{2,1,0:T(8,128)S(1)} %fusion.112), channel_id=1, source_target_pairs={{28,0},{0,4},{4,8},{8,12},{12,16},{16,20},{20,24},{24,28},{29,1},{... | collective-permute-start | bytes 393224 | tf_op jit(solution)/shard_map/while/body/eval_jaxpr/ppermute | solution.py:19
  88.5 6.9 %collective-permute-start = (bf16[1,36864]{1,0:T(2,128)(2,1)S(1)}, bf16[1,36864]{1,0:T(2,128)(2,1)S(1)}, u32[]{:S(2)}, u32[]{:S(2)}) collective-permute-start(bf16[1,36864]{1,0:T(2,128)(2,1)S(1)} %copy.35), channel_id=1, source_target_pairs={{28,0},{0,4},{4,8},{8,12},{12,16},{16,20},{20,24},{24,28},{29,1},{... | collective-permute-start | bytes 221192 | tf_op jit(solution)/shard_map/while/body/eval_jaxpr/ppermute | solution.py:19
  88.6 6.8 %collective-permute-start.1 = (f32[1,64]{1,0:T(1,128)S(1)}, f32[1,64]{1,0:T(1,128)S(1)}, u32[]{:S(2)}, u32[]{:S(2)}) collective-permute-start(f32[1,64]{1,0:T(1,128)S(1)} %get-tuple-element.299), channel_id=1, source_target_pairs={{28,0},{0,4},{4,8},{8,12},{12,16},{16,20},{20,24},{24,28},{29,1},{... | collective-permute-start | bytes 776 | tf_op jit(solution)/shard_map/while/body/eval_jaxpr/ppermute | solution.py:19
  89.0 6.4 %collective-permute-start.2 = (f32[1,64]{1,0:T(1,128)S(1)}, f32[1,64]{1,0:T(1,128)S(1)}, u32[]{:S(2)}, u32[]{:S(2)}) collective-permute-start(f32[1,64]{1,0:T(1,128)S(1)} %get-tuple-element.300), channel_id=1, source_target_pairs={{28,0},{0,4},{4,8},{8,12},{12,16},{16,20},{20,24},{24,28},{29,1},{... | collective-permute-start | bytes 776 | tf_op jit(solution)/shard_map/while/body/eval_jaxpr/ppermute | solution.py:19
  103.2 7.0 %collective-permute-start.3 = (f32[1,64,512]{2,1,0:T(8,128)S(1)}, f32[1,64,512]{2,1,0:T(8,128)}, u32[]{:S(2)}, u32[]{:S(2)}) collective-permute-start(f32[1,64,512]{2,1,0:T(8,128)S(1)} %fusion.112), channel_id=1, source_target_pairs={{28,0},{0,4},{4,8},{8,12},{12,16},{16,20},{20,24},{24,28},{29,1},{... | collective-permute-start | bytes 393224 | tf_op jit(solution)/shard_map/while/body/eval_jaxpr/ppermute | solution.py:19
  103.3 6.9 %collective-permute-start = (bf16[1,36864]{1,0:T(2,128)(2,1)S(1)}, bf16[1,36864]{1,0:T(2,128)(2,1)S(1)}, u32[]{:S(2)}, u32[]{:S(2)}) collective-permute-start(bf16[1,36864]{1,0:T(2,128)(2,1)S(1)} %copy.35), channel_id=1, source_target_pairs={{28,0},{0,4},{4,8},{8,12},{12,16},{16,20},{20,24},{24,28},{29,1},{... | collective-permute-start | bytes 221192 | tf_op jit(solution)/shard_map/while/body/eval_jaxpr/ppermute | solution.py:19
  103.4 6.8 %collective-permute-start.1 = (f32[1,64]{1,0:T(1,128)S(1)}, f32[1,64]{1,0:T(1,128)S(1)}, u32[]{:S(2)}, u32[]{:S(2)}) collective-permute-start(f32[1,64]{1,0:T(1,128)S(1)} %get-tuple-element.299), channel_id=1, source_target_pairs={{28,0},{0,4},{4,8},{8,12},{12,16},{16,20},{20,24},{24,28},{29,1},{... | collective-permute-start | bytes 776 | tf_op jit(solution)/shard_map/while/body/eval_jaxpr/ppermute | solution.py:19
  103.8 6.4 %collective-permute-start.2 = (f32[1,64]{1,0:T(1,128)S(1)}, f32[1,64]{1,0:T(1,128)S(1)}, u32[]{:S(2)}, u32[]{:S(2)}) collective-permute-start(f32[1,64]{1,0:T(1,128)S(1)} %get-tuple-element.300), channel_id=1, source_target_pairs={{28,0},{0,4},{4,8},{8,12},{12,16},{16,20},{20,24},{24,28},{29,1},{... | collective-permute-start | bytes 776 | tf_op jit(solution)/shard_map/while/body/eval_jaxpr/ppermute | solution.py:19
  118.0 7.0 %collective-permute-start.3 = (f32[1,64,512]{2,1,0:T(8,128)S(1)}, f32[1,64,512]{2,1,0:T(8,128)}, u32[]{:S(2)}, u32[]{:S(2)}) collective-permute-start(f32[1,64,512]{2,1,0:T(8,128)S(1)} %fusion.112), channel_id=1, source_target_pairs={{28,0},{0,4},{4,8},{8,12},{12,16},{16,20},{20,24},{24,28},{29,1},{... | collective-permute-start | bytes 393224 | tf_op jit(solution)/shard_map/while/body/eval_jaxpr/ppermute | solution.py:19
  118.1 6.9 %collective-permute-start = (bf16[1,36864]{1,0:T(2,128)(2,1)S(1)}, bf16[1,36864]{1,0:T(2,128)(2,1)S(1)}, u32[]{:S(2)}, u32[]{:S(2)}) collective-permute-start(bf16[1,36864]{1,0:T(2,128)(2,1)S(1)} %copy.35), channel_id=1, source_target_pairs={{28,0},{0,4},{4,8},{8,12},{12,16},{16,20},{20,24},{24,28},{29,1},{... | collective-permute-start | bytes 221192 | tf_op jit(solution)/shard_map/while/body/eval_jaxpr/ppermute | solution.py:19
  118.2 6.8 %collective-permute-start.1 = (f32[1,64]{1,0:T(1,128)S(1)}, f32[1,64]{1,0:T(1,128)S(1)}, u32[]{:S(2)}, u32[]{:S(2)}) collective-permute-start(f32[1,64]{1,0:T(1,128)S(1)} %get-tuple-element.299), channel_id=1, source_target_pairs={{28,0},{0,4},{4,8},{8,12},{12,16},{16,20},{20,24},{24,28},{29,1},{... | collective-permute-start | bytes 776 | tf_op jit(solution)/shard_map/while/body/eval_jaxpr/ppermute | solution.py:19
  118.6 6.4 %collective-permute-start.2 = (f32[1,64]{1,0:T(1,128)S(1)}, f32[1,64]{1,0:T(1,128)S(1)}, u32[]{:S(2)}, u32[]{:S(2)}) collective-permute-start(f32[1,64]{1,0:T(1,128)S(1)} %get-tuple-element.300), channel_id=1, source_target_pairs={{28,0},{0,4},{4,8},{8,12},{12,16},{16,20},{20,24},{24,28},{29,1},{... | collective-permute-start | bytes 776 | tf_op jit(solution)/shard_map/while/body/eval_jaxpr/ppermute | solution.py:19
  132.8 7.0 %collective-permute-start.3 = (f32[1,64,512]{2,1,0:T(8,128)S(1)}, f32[1,64,512]{2,1,0:T(8,128)}, u32[]{:S(2)}, u32[]{:S(2)}) collective-permute-start(f32[1,64,512]{2,1,0:T(8,128)S(1)} %fusion.112), channel_id=1, source_target_pairs={{28,0},{0,4},{4,8},{8,12},{12,16},{16,20},{20,24},{24,28},{29,1},{... | collective-permute-start | bytes 393224 | tf_op jit(solution)/shard_map/while/body/eval_jaxpr/ppermute | solution.py:19
  132.9 6.9 %collective-permute-start = (bf16[1,36864]{1,0:T(2,128)(2,1)S(1)}, bf16[1,36864]{1,0:T(2,128)(2,1)S(1)}, u32[]{:S(2)}, u32[]{:S(2)}) collective-permute-start(bf16[1,36864]{1,0:T(2,128)(2,1)S(1)} %copy.35), channel_id=1, source_target_pairs={{28,0},{0,4},{4,8},{8,12},{12,16},{16,20},{20,24},{24,28},{29,1},{... | collective-permute-start | bytes 221192 | tf_op jit(solution)/shard_map/while/body/eval_jaxpr/ppermute | solution.py:19
  133.0 6.8 %collective-permute-start.1 = (f32[1,64]{1,0:T(1,128)S(1)}, f32[1,64]{1,0:T(1,128)S(1)}, u32[]{:S(2)}, u32[]{:S(2)}) collective-permute-start(f32[1,64]{1,0:T(1,128)S(1)} %get-tuple-element.299), channel_id=1, source_target_pairs={{28,0},{0,4},{4,8},{8,12},{12,16},{16,20},{20,24},{24,28},{29,1},{... | collective-permute-start | bytes 776 | tf_op jit(solution)/shard_map/while/body/eval_jaxpr/ppermute | solution.py:19
  133.4 6.4 %collective-permute-start.2 = (f32[1,64]{1,0:T(1,128)S(1)}, f32[1,64]{1,0:T(1,128)S(1)}, u32[]{:S(2)}, u32[]{:S(2)}) collective-permute-start(f32[1,64]{1,0:T(1,128)S(1)} %get-tuple-element.300), channel_id=1, source_target_pairs={{28,0},{0,4},{4,8},{8,12},{12,16},{16,20},{20,24},{24,28},{29,1},{... | collective-permute-start | bytes 776 | tf_op jit(solution)/shard_map/while/body/eval_jaxpr/ppermute | solution.py:19
  146.1 8.6 %all-to-all-start = ((bf16[8,2,2048]{2,1,0:T(2,128)(2,1)}), bf16[8,2,2048]{2,1,0:T(2,128)(2,1)S(1)}, u32[]{:S(2)}, u32[]{:S(2)}) async-start(bf16[8,2,2048]{2,1,0:T(2,128)(2,1)} %reshape.378), calls=%async_computation | async-start | bytes 131072 | tf_op jit(solution)/shard_map/all_to_all | solution.py:135
  149.6 66.1 %all-reduce.3.cloned.1.call-start = ((), (), s32[]{:S(2)}) async-start(), calls=%async_computation.1 | async-start | bytes 229376
  (16 other events, 356.6 us)
Sparse Core Ops, SparseCore 0:
  164.3 51.3 all-reduce.2
where the time goes:
time: 225 us
  waiting for transfers between devices  79.8 us (35%)
  matrix products  68.6 us (30%)
  starting transfers between devices  36.3 us (16%)
  other arithmetic  16.6 us (7%)
  between operations  13.6 us (6%)
  local copies, waits for them, and re-layouts  9.15 us (4%)
    unnamed x2, waiting for transfers between devices  51 us
    ppermute x32, starting transfers between devices, passed_along(): return lax.ppermute(block, axis, route)  32.7 us
    dot_general x8, matrix products, prefix_part(): jnp.einsum('nhk,tk->nht', queries, prefix_cache, preferred_element_type=j...  28.8 us
    ppermute x32, waiting for transfers between devices, passed_along(): return lax.ppermute(block, axis, route)  23.9 us
    dot_general x8, matrix products, partial_softmax(): jnp.einsum('nht,tl->nhl', weights_low, values, preferred_element_type=jnp...  18.5 us
    dot_general x1, matrix products, on_device(): jnp.dot(head_out, out_weight, preferred_element_type=jnp.float32)  7.84 us
    broadcast_in_dim x8, other arithmetic, prefix_part(): jnp.broadcast_to((mask_rows > 0)[:, :, None], (count_rows, blocks_here, B...  5.6 us
    all_to_all x1, waiting for transfers between devices, on_device(): lax.all_to_all(context, 'blk', split_axis=1, concat_axis=0, tiled=True)  4.95 us
  transfers between devices with their start and end apart: 34, of which 10 were waited for; matrix products, arithmetic and copies ran while one was open for 0% of the time, Pallas kernels for 0%

commit v1 on v0

--- a/solution.py
+++ b/solution.py
@@ -132,7 +132,10 @@
     new_part = (new_scores, jnp.ones_like(new_scores), new_values)
     combined = combine_parts(combine_parts(prefix_result, suffix_result), new_part)
     context = (combined[2] / combined[1][..., None]).astype(jnp.bfloat16)
-    head_rows = lax.all_to_all(context, "blk", split_axis=1, concat_axis=0, tiled=True)
+    head_rows = jnp.concatenate(
+        lax.all_to_all(jnp.stack(jnp.split(context, lax.axis_size("blk"), axis=1)), "blk", 0, 0),
+        axis=0,
+    )
     head_out = jnp.einsum("rhl,hlv->rhv", head_rows, value_up, preferred_element_type=jnp.float32)
     head_out = head_out.astype(jnp.bfloat16).reshape(group_rows, -1)
     group_hit = (tenant_ids[:, None] == jnp.arange(tenants)[None, :]).astype(jnp.float32)

time: 225 us -> 228 us (1.013)
  local copies, waits for them, and re-layouts: 9.15 us -> 12.6 us
    unnamed x18 -> x21, local copies, waits for them, and re-layouts: 3.96 us -> 6.87 us
where the time goes in v1:
time: 228 us; the launch traced here: 227 us
  waiting for transfers between devices  79.8 us (35%)
  matrix products  68.6 us (30%)
  starting transfers between devices  36.3 us (16%)
  other arithmetic  15.6 us (7%)
  between operations  13.5 us (6%)
  local copies, waits for them, and re-layouts  12.6 us (6%)
    unnamed x2, waiting for transfers between devices  51 us
    ppermute x32, starting transfers between devices, passed_along(): return lax.ppermute(block, axis, route)  32.7 us
    dot_general x8, matrix products, prefix_part(): jnp.einsum('nhk,tk->nht', queries, prefix_cache, preferred_element_type=j...  28.8 us
    ppermute x32, waiting for transfers between devices, passed_along(): return lax.ppermute(block, axis, route)  23.9 us
    dot_general x8, matrix products, partial_softmax(): jnp.einsum('nht,tl->nhl', weights_low, values, preferred_element_type=jnp...  18.5 us
    dot_general x1, matrix products, on_device(): jnp.dot(head_out, out_weight, preferred_element_type=jnp.float32)  7.84 us
    unnamed x21, local copies, waits for them, and re-layouts  6.87 us
    broadcast_in_dim x8, other arithmetic, prefix_part(): jnp.broadcast_to((mask_rows > 0)[:, :, None], (count_rows, blocks_here, B...  5.6 us
  transfers between devices with their start and end apart: 34, of which 10 were waited for; matrix products, arithmetic and copies ran while one was open for 0% of the time, Pallas kernels for 0%

profile of v1, /device:TPU:0, one launch (start us, length us, event | category | flops | bytes accessed | tf_op | source)
XLA Modules:
  0.0 227.1 jit_solution(130158430245078308)
XLA Ops:
  12.9 3.2 %fusion.80 = (bf16[36864]{0:T(1024)(128)(2,1)S(1)}, bf16[1,36864]{1,0:T(2,128)(2,1)S(1)}) fusion(bf16[64,1]{0,1:T(2,128)(2,1)S(1)} %reshape.367, bf16[64,36864]{1,0:T(8,128)(2,1)} %bitcast.208, bf16[1,36864]{1,0:T(2,128)(2,1)} %param.16), kind=kOutput, calls=%fused_computation.101 | convolution fusion | flops 4829184 | bytes 4939904 | tf_op jit(solution)/shard_map/dot_general | solution.py:96
  16.2 3.5 %fusion.82 = (f32[64]{0:T(128)S(1)}, f32[64,4096]{1,0:T(8,128)S(1)}) fusion(bf16[64,576]{1,0:T(8,128)(2,1)S(1)} %reshape.358, bf16[1,4096,576]{1,2,0:T(8,128)(2,1)} %param.23, pred[4096]{0:T(1024)(128)(4,1)S(1)} %iota_compare_fusion), kind=kOutput, calls=%fused_computation.103 | convolution fusion | flops 302776256 | bytes 5845248 | tf_op jit(solution)/shard_map/nhk,ntk->nht/dot_general | solution.py:120
  20.7 119.1 %while.21 = (s32[]{:T(128)}, bf16[1,36864]{1,0:T(2,128)(2,1)S(1)}, f32[1,64]{1,0:T(1,128)S(1)}, f32[1,64]{1,0:T(1,128)S(1)}, f32[1,64,512]{2,1,0:T(8,128)}, /*in...) while((s32[]{:T(128)}, bf16[1,36864]{1,0:T(2,128)(2,1)S(1)}, ...), condition=%wide.region_4.5_spmd, body=%wide.region_1.4_spmd.sunk | while | flops 572359104 | bytes 32546200 | solution.py:114
  22.2 3.6 %fusion.109 = (f32[64]{0:T(128)S(1)}, f32[64,4096]{1,0:T(8,128)S(1)}) fusion(bf16[64,576]{1,0:T(8,128)(2,1)S(1)} %reshape.380, bf16[4096,576]{0,1:T(8,128)(2,1)} %get-tuple-element.336, pred[4096]{0:T(1024)(128)(4,1)S(1)} %broadcast_bitcast_fusion.2), kind=kOutput, calls=%fused_computation.100.clone.1 | convolution fusion | flops 302776256 | bytes 5845248 | tf_op jit(solution)/shard_map/while/body/eval_jaxpr/nhk,tk->nht/dot_general | solution.py:48
  29.0 2.6 %collective-permute-start = (bf16[1,36864]{1,0:T(2,128)(2,1)S(1)}, bf16[1,36864]{1,0:T(2,128)(2,1)S(1)}, u32[]{:S(2)}, u32[]{:S(2)}) collective-permute-start(bf16[1,36864]{1,0:T(2,128)(2,1)S(1)} %copy.27), channel_id=1, source_target_pairs={{28,0},{0,4},{4,8},{8,12},{12,16},{16,20},{20,24},{24,28},{29,1},{... | collective-permute-start | bytes 221192 | tf_op jit(solution)/shard_map/while/body/eval_jaxpr/ppermute | solution.py:19
  33.2 3.0 %collective-permute-done.1 = f32[1,64]{1,0:T(1,128)S(1)} collective-permute-done((f32[1,64]{1,0:T(1,128)S(1)}, f32[1,64]{1,0:T(1,128)S(1)}, u32[]{:S(2)}, u32[]{:S(2)}) %collective-permute-start.1) | collective-permute-done | bytes 288 | tf_op jit(solution)/shard_map/while/body/eval_jaxpr/ppermute | solution.py:19
  37.7 3.6 %fusion.109 = (f32[64]{0:T(128)S(1)}, f32[64,4096]{1,0:T(8,128)S(1)}) fusion(bf16[64,576]{1,0:T(8,128)(2,1)S(1)} %reshape.380, bf16[4096,576]{0,1:T(8,128)(2,1)} %get-tuple-element.336, pred[4096]{0:T(1024)(128)(4,1)S(1)} %broadcast_bitcast_fusion.2), kind=kOutput, calls=%fused_computation.100.clone.1 | convolution fusion | flops 302776256 | bytes 5845248 | tf_op jit(solution)/shard_map/while/body/eval_jaxpr/nhk,tk->nht/dot_general | solution.py:48
  45.6 2.4 %collective-permute-start.2 = (f32[1,64]{1,0:T(1,128)S(1)}, f32[1,64]{1,0:T(1,128)S(1)}, u32[]{:S(2)}, u32[]{:S(2)}) collective-permute-start(f32[1,64]{1,0:T(1,128)S(1)} %get-tuple-element.300), channel_id=1, source_target_pairs={{28,0},{0,4},{4,8},{8,12},{12,16},{16,20},{20,24},{24,28},{29,1},{... | collective-permute-start | bytes 776 | tf_op jit(solution)/shard_map/while/body/eval_jaxpr/ppermute | solution.py:19
  48.0 3.0 %collective-permute-done.1 = f32[1,64]{1,0:T(1,128)S(1)} collective-permute-done((f32[1,64]{1,0:T(1,128)S(1)}, f32[1,64]{1,0:T(1,128)S(1)}, u32[]{:S(2)}, u32[]{:S(2)}) %collective-permute-start.1) | collective-permute-done | bytes 288 | tf_op jit(solution)/shard_map/while/body/eval_jaxpr/ppermute | solution.py:19
  52.5 3.6 %fusion.109 = (f32[64]{0:T(128)S(1)}, f32[64,4096]{1,0:T(8,128)S(1)}) fusion(bf16[64,576]{1,0:T(8,128)(2,1)S(1)} %reshape.380, bf16[4096,576]{0,1:T(8,128)(2,1)} %get-tuple-element.336, pred[4096]{0:T(1024)(128)(4,1)S(1)} %broadcast_bitcast_fusion.2), kind=kOutput, calls=%fused_computation.100.clone.1 | convolution fusion | flops 302776256 | bytes 5845248 | tf_op jit(solution)/shard_map/while/body/eval_jaxpr/nhk,tk->nht/dot_general | solution.py:48
  59.5 3.3 %collective-permute-start.2 = (f32[1,64]{1,0:T(1,128)S(1)}, f32[1,64]{1,0:T(1,128)S(1)}, u32[]{:S(2)}, u32[]{:S(2)}) collective-permute-start(f32[1,64]{1,0:T(1,128)S(1)} %get-tuple-element.300), channel_id=1, source_target_pairs={{28,0},{0,4},{4,8},{8,12},{12,16},{16,20},{20,24},{24,28},{29,1},{... | collective-permute-start | bytes 776 | tf_op jit(solution)/shard_map/while/body/eval_jaxpr/ppermute | solution.py:19
  62.8 3.0 %collective-permute-done.1 = f32[1,64]{1,0:T(1,128)S(1)} collective-permute-done((f32[1,64]{1,0:T(1,128)S(1)}, f32[1,64]{1,0:T(1,128)S(1)}, u32[]{:S(2)}, u32[]{:S(2)}) %collective-permute-start.1) | collective-permute-done | bytes 288 | tf_op jit(solution)/shard_map/while/body/eval_jaxpr/ppermute | solution.py:19
  67.3 3.6 %fusion.109 = (f32[64]{0:T(128)S(1)}, f32[64,4096]{1,0:T(8,128)S(1)}) fusion(bf16[64,576]{1,0:T(8,128)(2,1)S(1)} %reshape.380, bf16[4096,576]{0,1:T(8,128)(2,1)} %get-tuple-element.336, pred[4096]{0:T(1024)(128)(4,1)S(1)} %broadcast_bitcast_fusion.2), kind=kOutput, calls=%fused_computation.100.clone.1 | convolution fusion | flops 302776256 | bytes 5845248 | tf_op jit(solution)/shard_map/while/body/eval_jaxpr/nhk,tk->nht/dot_general | solution.py:48
  74.2 3.4 %collective-permute-start.2 = (f32[1,64]{1,0:T(1,128)S(1)}, f32[1,64]{1,0:T(1,128)S(1)}, u32[]{:S(2)}, u32[]{:S(2)}) collective-permute-start(f32[1,64]{1,0:T(1,128)S(1)} %get-tuple-element.300), channel_id=1, source_target_pairs={{28,0},{0,4},{4,8},{8,12},{12,16},{16,20},{20,24},{24,28},{29,1},{... | collective-permute-start | bytes 776 | tf_op jit(solution)/shard_map/while/body/eval_jaxpr/ppermute | solution.py:19
  77.6 3.0 %collective-permute-done.1 = f32[1,64]{1,0:T(1,128)S(1)} collective-permute-done((f32[1,64]{1,0:T(1,128)S(1)}, f32[1,64]{1,0:T(1,128)S(1)}, u32[]{:S(2)}, u32[]{:S(2)}) %collective-permute-start.1) | collective-permute-done | bytes 288 | tf_op jit(solution)/shard_map/while/body/eval_jaxpr/ppermute | solution.py:19
  82.1 3.6 %fusion.109 = (f32[64]{0:T(128)S(1)}, f32[64,4096]{1,0:T(8,128)S(1)}) fusion(bf16[64,576]{1,0:T(8,128)(2,1)S(1)} %reshape.380, bf16[4096,576]{0,1:T(8,128)(2,1)} %get-tuple-element.336, pred[4096]{0:T(1024)(128)(4,1)S(1)} %broadcast_bitcast_fusion.2), kind=kOutput, calls=%fused_computation.100.clone.1 | convolution fusion | flops 302776256 | bytes 5845248 | tf_op jit(solution)/shard_map/while/body/eval_jaxpr/nhk,tk->nht/dot_general | solution.py:48
  89.0 3.4 %collective-permute-start.2 = (f32[1,64]{1,0:T(1,128)S(1)}, f32[1,64]{1,0:T(1,128)S(1)}, u32[]{:S(2)}, u32[]{:S(2)}) collective-permute-start(f32[1,64]{1,0:T(1,128)S(1)} %get-tuple-element.300), channel_id=1, source_target_pairs={{28,0},{0,4},{4,8},{8,12},{12,16},{16,20},{20,24},{24,28},{29,1},{... | collective-permute-start | bytes 776 | tf_op jit(solution)/shard_map/while/body/eval_jaxpr/ppermute | solution.py:19
  92.4 3.0 %collective-permute-done.1 = f32[1,64]{1,0:T(1,128)S(1)} collective-permute-done((f32[1,64]{1,0:T(1,128)S(1)}, f32[1,64]{1,0:T(1,128)S(1)}, u32[]{:S(2)}, u32[]{:S(2)}) %collective-permute-start.1) | collective-permute-done | bytes 288 | tf_op jit(solution)/shard_map/while/body/eval_jaxpr/ppermute | solution.py:19
  96.9 3.6 %fusion.109 = (f32[64]{0:T(128)S(1)}, f32[64,4096]{1,0:T(8,128)S(1)}) fusion(bf16[64,576]{1,0:T(8,128)(2,1)S(1)} %reshape.380, bf16[4096,576]{0,1:T(8,128)(2,1)} %get-tuple-element.336, pred[4096]{0:T(1024)(128)(4,1)S(1)} %broadcast_bitcast_fusion.2), kind=kOutput, calls=%fused_computation.100.clone.1 | convolution fusion | flops 302776256 | bytes 5845248 | tf_op jit(solution)/shard_map/while/body/eval_jaxpr/nhk,tk->nht/dot_general | solution.py:48
  103.8 3.4 %collective-permute-start.2 = (f32[1,64]{1,0:T(1,128)S(1)}, f32[1,64]{1,0:T(1,128)S(1)}, u32[]{:S(2)}, u32[]{:S(2)}) collective-permute-start(f32[1,64]{1,0:T(1,128)S(1)} %get-tuple-element.300), channel_id=1, source_target_pairs={{28,0},{0,4},{4,8},{8,12},{12,16},{16,20},{20,24},{24,28},{29,1},{... | collective-permute-start | bytes 776 | tf_op jit(solution)/shard_map/while/body/eval_jaxpr/ppermute | solution.py:19
  107.2 3.0 %collective-permute-done.1 = f32[1,64]{1,0:T(1,128)S(1)} collective-permute-done((f32[1,64]{1,0:T(1,128)S(1)}, f32[1,64]{1,0:T(1,128)S(1)}, u32[]{:S(2)}, u32[]{:S(2)}) %collective-permute-start.1) | collective-permute-done | bytes 288 | tf_op jit(solution)/shard_map/while/body/eval_jaxpr/ppermute | solution.py:19
  111.7 3.6 %fusion.109 = (f32[64]{0:T(128)S(1)}, f32[64,4096]{1,0:T(8,128)S(1)}) fusion(bf16[64,576]{1,0:T(8,128)(2,1)S(1)} %reshape.380, bf16[4096,576]{0,1:T(8,128)(2,1)} %get-tuple-element.336, pred[4096]{0:T(1024)(128)(4,1)S(1)} %broadcast_bitcast_fusion.2), kind=kOutput, calls=%fused_computation.100.clone.1 | convolution fusion | flops 302776256 | bytes 5845248 | tf_op jit(solution)/shard_map/while/body/eval_jaxpr/nhk,tk->nht/dot_general | solution.py:48
  118.6 3.4 %collective-permute-start.2 = (f32[1,64]{1,0:T(1,128)S(1)}, f32[1,64]{1,0:T(1,128)S(1)}, u32[]{:S(2)}, u32[]{:S(2)}) collective-permute-start(f32[1,64]{1,0:T(1,128)S(1)} %get-tuple-element.300), channel_id=1, source_target_pairs={{28,0},{0,4},{4,8},{8,12},{12,16},{16,20},{20,24},{24,28},{29,1},{... | collective-permute-start | bytes 776 | tf_op jit(solution)/shard_map/while/body/eval_jaxpr/ppermute | solution.py:19
  122.0 3.0 %collective-permute-done.1 = f32[1,64]{1,0:T(1,128)S(1)} collective-permute-done((f32[1,64]{1,0:T(1,128)S(1)}, f32[1,64]{1,0:T(1,128)S(1)}, u32[]{:S(2)}, u32[]{:S(2)}) %collective-permute-start.1) | collective-permute-done | bytes 288 | tf_op jit(solution)/shard_map/while/body/eval_jaxpr/ppermute | solution.py:19
  126.5 3.6 %fusion.109 = (f32[64]{0:T(128)S(1)}, f32[64,4096]{1,0:T(8,128)S(1)}) fusion(bf16[64,576]{1,0:T(8,128)(2,1)S(1)} %reshape.380, bf16[4096,576]{0,1:T(8,128)(2,1)} %get-tuple-element.336, pred[4096]{0:T(1024)(128)(4,1)S(1)} %broadcast_bitcast_fusion.2), kind=kOutput, calls=%fused_computation.100.clone.1 | convolution fusion | flops 302776256 | bytes 5845248 | tf_op jit(solution)/shard_map/while/body/eval_jaxpr/nhk,tk->nht/dot_general | solution.py:48
  133.4 3.4 %collective-permute-start.2 = (f32[1,64]{1,0:T(1,128)S(1)}, f32[1,64]{1,0:T(1,128)S(1)}, u32[]{:S(2)}, u32[]{:S(2)}) collective-permute-start(f32[1,64]{1,0:T(1,128)S(1)} %get-tuple-element.300), channel_id=1, source_target_pairs={{28,0},{0,4},{4,8},{8,12},{12,16},{16,20},{20,24},{24,28},{29,1},{... | collective-permute-start | bytes 776 | tf_op jit(solution)/shard_map/while/body/eval_jaxpr/ppermute | solution.py:19
  136.8 3.0 %collective-permute-done.1 = f32[1,64]{1,0:T(1,128)S(1)} collective-permute-done((f32[1,64]{1,0:T(1,128)S(1)}, f32[1,64]{1,0:T(1,128)S(1)}, u32[]{:S(2)}, u32[]{:S(2)}) %collective-permute-start.1) | collective-permute-done | bytes 288 | tf_op jit(solution)/shard_map/while/body/eval_jaxpr/ppermute | solution.py:19
  140.0 3.8 %fusion.53 = bf16[1,64,512]{2,1,0:T(8,128)(2,1)S(1)} fusion(bf16[1,4096,576]{1,2,0:T(8,128)(2,1)} %param.23, f32[64,4096]{1,0:T(8,128)S(1)} %get-tuple-element.239, f32[64]{0:T(128)S(1)} %broadcast_maximum_fusion.1, f32[1,64,512]{2,1,0:T(8,128)} %get-tuple-element.206, f32[64]{0:T(128)S(1)} %get-tuple-element.232, f32[64]{0:T(128)S(1)} %get-tuple-element.233, ...), kind=kOutput, calls=%fused_computation.45 | convolution fusion | flops 269221888 | bytes 5443072 | tf_op jit(solution)/shard_map/nht,ntl->nhl/dot_general | solution.py:38
  148.6 3.5 %all-to-all-start = ((bf16[8,1,8,512]{3,2,1,0:T(8,128)(2,1)}), bf16[8,1,8,512]{3,2,1,0:T(8,128)(2,1)S(1)}, u32[]{:S(2)}, u32[]{:S(2)}) async-start(bf16[8,1,8,512]{3,2,1,0:T(8,128)(2,1)} %constant_dynamic-update-slice_fusion), calls=%async_computation | async-start | bytes 131072 | tf_op jit(solution)/shard_map/all_to_all | solution.py:136
  152.2 5.0 %all-to-all-done = bf16[8,1,8,512]{3,2,1,0:T(8,128)(2,1)S(1)} async-done(((bf16[8,1,8,512]{3,2,1,0:T(8,128)(2,1)}), bf16[8,1,8,512]{3,2,1,0:T(8,128)(2,1)S(1)}, u32[]{:S(2)}, u32[]{:S(2)}) %all-to-all-start) | async-done | bytes 65568 | tf_op jit(solution)/shard_map/all_to_all | solution.py:136
  158.7 7.8 %fusion.21 = bf16[8,7168]{1,0:T(8,128)(2,1)} fusion(f32[8,7168]{1,0:T(8,128)S(1)} %convolution_bitcast_fusion, bf16[1024,7168]{1,0:T(8,128)(2,1)} %param.27, bf16[8,8,128]{2,1,0:T(8,128)(2,1)S(1)} %convolution_convert_fusion), kind=kOutput, calls=%fused_computation.26 | convolution fusion | flops 117555200 | bytes 15040512 | tf_op jit(solution)/shard_map/dot_general | solution.py:143
  167.2 50.9 %all-reduce.3.cloned.1.call-done = bf16[8,7168]{1,0:T(8,128)(2,1)} async-done(((bf16[8,7168]{1,0:T(8,128)(2,1)}), bf16[8,7168]{1,0:T(8,128)(2,1)}) %all-reduce.3.cloned.1.call-update) | async-done | bytes 114704
  (180 shorter events, 57.1 us)
Async XLA Ops:
  28.5 7.7 %collective-permute-start.3 = (f32[1,64,512]{2,1,0:T(8,128)S(1)}, f32[1,64,512]{2,1,0:T(8,128)}, u32[]{:S(2)}, u32[]{:S(2)}) collective-permute-start(f32[1,64,512]{2,1,0:T(8,128)S(1)} %fusion.112), channel_id=1, source_target_pairs={{28,0},{0,4},{4,8},{8,12},{12,16},{16,20},{20,24},{24,28},{29,1},{... | collective-permute-start | bytes 393224 | tf_op jit(solution)/shard_map/while/body/eval_jaxpr/ppermute | solution.py:19
  29.0 7.2 %collective-permute-start = (bf16[1,36864]{1,0:T(2,128)(2,1)S(1)}, bf16[1,36864]{1,0:T(2,128)(2,1)S(1)}, u32[]{:S(2)}, u32[]{:S(2)}) collective-permute-start(bf16[1,36864]{1,0:T(2,128)(2,1)S(1)} %copy.27), channel_id=1, source_target_pairs={{28,0},{0,4},{4,8},{8,12},{12,16},{16,20},{20,24},{24,28},{29,1},{... | collective-permute-start | bytes 221192 | tf_op jit(solution)/shard_map/while/body/eval_jaxpr/ppermute | solution.py:19
  44.0 7.0 %collective-permute-start.3 = (f32[1,64,512]{2,1,0:T(8,128)S(1)}, f32[1,64,512]{2,1,0:T(8,128)}, u32[]{:S(2)}, u32[]{:S(2)}) collective-permute-start(f32[1,64,512]{2,1,0:T(8,128)S(1)} %fusion.112), channel_id=1, source_target_pairs={{28,0},{0,4},{4,8},{8,12},{12,16},{16,20},{20,24},{24,28},{29,1},{... | collective-permute-start | bytes 393224 | tf_op jit(solution)/shard_map/while/body/eval_jaxpr/ppermute | solution.py:19
  44.1 6.9 %collective-permute-start = (bf16[1,36864]{1,0:T(2,128)(2,1)S(1)}, bf16[1,36864]{1,0:T(2,128)(2,1)S(1)}, u32[]{:S(2)}, u32[]{:S(2)}) collective-permute-start(bf16[1,36864]{1,0:T(2,128)(2,1)S(1)} %copy.27), channel_id=1, source_target_pairs={{28,0},{0,4},{4,8},{8,12},{12,16},{16,20},{20,24},{24,28},{29,1},{... | collective-permute-start | bytes 221192 | tf_op jit(solution)/shard_map/while/body/eval_jaxpr/ppermute | solution.py:19
  45.5 5.5 %collective-permute-start.1 = (f32[1,64]{1,0:T(1,128)S(1)}, f32[1,64]{1,0:T(1,128)S(1)}, u32[]{:S(2)}, u32[]{:S(2)}) collective-permute-start(f32[1,64]{1,0:T(1,128)S(1)} %get-tuple-element.299), channel_id=1, source_target_pairs={{28,0},{0,4},{4,8},{8,12},{12,16},{16,20},{20,24},{24,28},{29,1},{... | collective-permute-start | bytes 776 | tf_op jit(solution)/shard_map/while/body/eval_jaxpr/ppermute | solution.py:19
  45.6 5.4 %collective-permute-start.2 = (f32[1,64]{1,0:T(1,128)S(1)}, f32[1,64]{1,0:T(1,128)S(1)}, u32[]{:S(2)}, u32[]{:S(2)}) collective-permute-start(f32[1,64]{1,0:T(1,128)S(1)} %get-tuple-element.300), channel_id=1, source_target_pairs={{28,0},{0,4},{4,8},{8,12},{12,16},{16,20},{20,24},{24,28},{29,1},{... | collective-permute-start | bytes 776 | tf_op jit(solution)/shard_map/while/body/eval_jaxpr/ppermute | solution.py:19
  58.8 7.0 %collective-permute-start.3 = (f32[1,64,512]{2,1,0:T(8,128)S(1)}, f32[1,64,512]{2,1,0:T(8,128)}, u32[]{:S(2)}, u32[]{:S(2)}) collective-permute-start(f32[1,64,512]{2,1,0:T(8,128)S(1)} %fusion.112), channel_id=1, source_target_pairs={{28,0},{0,4},{4,8},{8,12},{12,16},{16,20},{20,24},{24,28},{29,1},{... | collective-permute-start | bytes 393224 | tf_op jit(solution)/shard_map/while/body/eval_jaxpr/ppermute | solution.py:19
  58.9 6.9 %collective-permute-start = (bf16[1,36864]{1,0:T(2,128)(2,1)S(1)}, bf16[1,36864]{1,0:T(2,128)(2,1)S(1)}, u32[]{:S(2)}, u32[]{:S(2)}) collective-permute-start(bf16[1,36864]{1,0:T(2,128)(2,1)S(1)} %copy.27), channel_id=1, source_target_pairs={{28,0},{0,4},{4,8},{8,12},{12,16},{16,20},{20,24},{24,28},{29,1},{... | collective-permute-start | bytes 221192 | tf_op jit(solution)/shard_map/while/body/eval_jaxpr/ppermute | solution.py:19
  59.4 6.4 %collective-permute-start.1 = (f32[1,64]{1,0:T(1,128)S(1)}, f32[1,64]{1,0:T(1,128)S(1)}, u32[]{:S(2)}, u32[]{:S(2)}) collective-permute-start(f32[1,64]{1,0:T(1,128)S(1)} %get-tuple-element.299), channel_id=1, source_target_pairs={{28,0},{0,4},{4,8},{8,12},{12,16},{16,20},{20,24},{24,28},{29,1},{... | collective-permute-start | bytes 776 | tf_op jit(solution)/shard_map/while/body/eval_jaxpr/ppermute | solution.py:19
  59.5 6.3 %collective-permute-start.2 = (f32[1,64]{1,0:T(1,128)S(1)}, f32[1,64]{1,0:T(1,128)S(1)}, u32[]{:S(2)}, u32[]{:S(2)}) collective-permute-start(f32[1,64]{1,0:T(1,128)S(1)} %get-tuple-element.300), channel_id=1, source_target_pairs={{28,0},{0,4},{4,8},{8,12},{12,16},{16,20},{20,24},{24,28},{29,1},{... | collective-permute-start | bytes 776 | tf_op jit(solution)/shard_map/while/body/eval_jaxpr/ppermute | solution.py:19
  73.6 7.0 %collective-permute-start.3 = (f32[1,64,512]{2,1,0:T(8,128)S(1)}, f32[1,64,512]{2,1,0:T(8,128)}, u32[]{:S(2)}, u32[]{:S(2)}) collective-permute-start(f32[1,64,512]{2,1,0:T(8,128)S(1)} %fusion.112), channel_id=1, source_target_pairs={{28,0},{0,4},{4,8},{8,12},{12,16},{16,20},{20,24},{24,28},{29,1},{... | collective-permute-start | bytes 393224 | tf_op jit(solution)/shard_map/while/body/eval_jaxpr/ppermute | solution.py:19
  73.7 6.9 %collective-permute-start = (bf16[1,36864]{1,0:T(2,128)(2,1)S(1)}, bf16[1,36864]{1,0:T(2,128)(2,1)S(1)}, u32[]{:S(2)}, u32[]{:S(2)}) collective-permute-start(bf16[1,36864]{1,0:T(2,128)(2,1)S(1)} %copy.27), channel_id=1, source_target_pairs={{28,0},{0,4},{4,8},{8,12},{12,16},{16,20},{20,24},{24,28},{29,1},{... | collective-permute-start | bytes 221192 | tf_op jit(solution)/shard_map/while/body/eval_jaxpr/ppermute | solution.py:19
  73.7 6.8 %collective-permute-start.1 = (f32[1,64]{1,0:T(1,128)S(1)}, f32[1,64]{1,0:T(1,128)S(1)}, u32[]{:S(2)}, u32[]{:S(2)}) collective-permute-start(f32[1,64]{1,0:T(1,128)S(1)} %get-tuple-element.299), channel_id=1, source_target_pairs={{28,0},{0,4},{4,8},{8,12},{12,16},{16,20},{20,24},{24,28},{29,1},{... | collective-permute-start | bytes 776 | tf_op jit(solution)/shard_map/while/body/eval_jaxpr/ppermute | solution.py:19
  74.2 6.4 %collective-permute-start.2 = (f32[1,64]{1,0:T(1,128)S(1)}, f32[1,64]{1,0:T(1,128)S(1)}, u32[]{:S(2)}, u32[]{:S(2)}) collective-permute-start(f32[1,64]{1,0:T(1,128)S(1)} %get-tuple-element.300), channel_id=1, source_target_pairs={{28,0},{0,4},{4,8},{8,12},{12,16},{16,20},{20,24},{24,28},{29,1},{... | collective-permute-start | bytes 776 | tf_op jit(solution)/shard_map/while/body/eval_jaxpr/ppermute | solution.py:19
  88.4 7.0 %collective-permute-start.3 = (f32[1,64,512]{2,1,0:T(8,128)S(1)}, f32[1,64,512]{2,1,0:T(8,128)}, u32[]{:S(2)}, u32[]{:S(2)}) collective-permute-start(f32[1,64,512]{2,1,0:T(8,128)S(1)} %fusion.112), channel_id=1, source_target_pairs={{28,0},{0,4},{4,8},{8,12},{12,16},{16,20},{20,24},{24,28},{29,1},{... | collective-permute-start | bytes 393224 | tf_op jit(solution)/shard_map/while/body/eval_jaxpr/ppermute | solution.py:19
  88.5 6.9 %collective-permute-start = (bf16[1,36864]{1,0:T(2,128)(2,1)S(1)}, bf16[1,36864]{1,0:T(2,128)(2,1)S(1)}, u32[]{:S(2)}, u32[]{:S(2)}) collective-permute-start(bf16[1,36864]{1,0:T(2,128)(2,1)S(1)} %copy.27), channel_id=1, source_target_pairs={{28,0},{0,4},{4,8},{8,12},{12,16},{16,20},{20,24},{24,28},{29,1},{... | collective-permute-start | bytes 221192 | tf_op jit(solution)/shard_map/while/body/eval_jaxpr/ppermute | solution.py:19
  88.6 6.8 %collective-permute-start.1 = (f32[1,64]{1,0:T(1,128)S(1)}, f32[1,64]{1,0:T(1,128)S(1)}, u32[]{:S(2)}, u32[]{:S(2)}) collective-permute-start(f32[1,64]{1,0:T(1,128)S(1)} %get-tuple-element.299), channel_id=1, source_target_pairs={{28,0},{0,4},{4,8},{8,12},{12,16},{16,20},{20,24},{24,28},{29,1},{... | collective-permute-start | bytes 776 | tf_op jit(solution)/shard_map/while/body/eval_jaxpr/ppermute | solution.py:19
  89.0 6.4 %collective-permute-start.2 = (f32[1,64]{1,0:T(1,128)S(1)}, f32[1,64]{1,0:T(1,128)S(1)}, u32[]{:S(2)}, u32[]{:S(2)}) collective-permute-start(f32[1,64]{1,0:T(1,128)S(1)} %get-tuple-element.300), channel_id=1, source_target_pairs={{28,0},{0,4},{4,8},{8,12},{12,16},{16,20},{20,24},{24,28},{29,1},{... | collective-permute-start | bytes 776 | tf_op jit(solution)/shard_map/while/body/eval_jaxpr/ppermute | solution.py:19
  103.2 7.0 %collective-permute-start.3 = (f32[1,64,512]{2,1,0:T(8,128)S(1)}, f32[1,64,512]{2,1,0:T(8,128)}, u32[]{:S(2)}, u32[]{:S(2)}) collective-permute-start(f32[1,64,512]{2,1,0:T(8,128)S(1)} %fusion.112), channel_id=1, source_target_pairs={{28,0},{0,4},{4,8},{8,12},{12,16},{16,20},{20,24},{24,28},{29,1},{... | collective-permute-start | bytes 393224 | tf_op jit(solution)/shard_map/while/body/eval_jaxpr/ppermute | solution.py:19
  103.3 6.9 %collective-permute-start = (bf16[1,36864]{1,0:T(2,128)(2,1)S(1)}, bf16[1,36864]{1,0:T(2,128)(2,1)S(1)}, u32[]{:S(2)}, u32[]{:S(2)}) collective-permute-start(bf16[1,36864]{1,0:T(2,128)(2,1)S(1)} %copy.27), channel_id=1, source_target_pairs={{28,0},{0,4},{4,8},{8,12},{12,16},{16,20},{20,24},{24,28},{29,1},{... | collective-permute-start | bytes 221192 | tf_op jit(solution)/shard_map/while/body/eval_jaxpr/ppermute | solution.py:19
  103.4 6.8 %collective-permute-start.1 = (f32[1,64]{1,0:T(1,128)S(1)}, f32[1,64]{1,0:T(1,128)S(1)}, u32[]{:S(2)}, u32[]{:S(2)}) collective-permute-start(f32[1,64]{1,0:T(1,128)S(1)} %get-tuple-element.299), channel_id=1, source_target_pairs={{28,0},{0,4},{4,8},{8,12},{12,16},{16,20},{20,24},{24,28},{29,1},{... | collective-permute-start | bytes 776 | tf_op jit(solution)/shard_map/while/body/eval_jaxpr/ppermute | solution.py:19
  103.8 6.4 %collective-permute-start.2 = (f32[1,64]{1,0:T(1,128)S(1)}, f32[1,64]{1,0:T(1,128)S(1)}, u32[]{:S(2)}, u32[]{:S(2)}) collective-permute-start(f32[1,64]{1,0:T(1,128)S(1)} %get-tuple-element.300), channel_id=1, source_target_pairs={{28,0},{0,4},{4,8},{8,12},{12,16},{16,20},{20,24},{24,28},{29,1},{... | collective-permute-start | bytes 776 | tf_op jit(solution)/shard_map/while/body/eval_jaxpr/ppermute | solution.py:19
  118.0 7.0 %collective-permute-start.3 = (f32[1,64,512]{2,1,0:T(8,128)S(1)}, f32[1,64,512]{2,1,0:T(8,128)}, u32[]{:S(2)}, u32[]{:S(2)}) collective-permute-start(f32[1,64,512]{2,1,0:T(8,128)S(1)} %fusion.112), channel_id=1, source_target_pairs={{28,0},{0,4},{4,8},{8,12},{12,16},{16,20},{20,24},{24,28},{29,1},{... | collective-permute-start | bytes 393224 | tf_op jit(solution)/shard_map/while/body/eval_jaxpr/ppermute | solution.py:19
  118.1 6.9 %collective-permute-start = (bf16[1,36864]{1,0:T(2,128)(2,1)S(1)}, bf16[1,36864]{1,0:T(2,128)(2,1)S(1)}, u32[]{:S(2)}, u32[]{:S(2)}) collective-permute-start(bf16[1,36864]{1,0:T(2,128)(2,1)S(1)} %copy.27), channel_id=1, source_target_pairs={{28,0},{0,4},{4,8},{8,12},{12,16},{16,20},{20,24},{24,28},{29,1},{... | collective-permute-start | bytes 221192 | tf_op jit(solution)/shard_map/while/body/eval_jaxpr/ppermute | solution.py:19
  118.2 6.8 %collective-permute-start.1 = (f32[1,64]{1,0:T(1,128)S(1)}, f32[1,64]{1,0:T(1,128)S(1)}, u32[]{:S(2)}, u32[]{:S(2)}) collective-permute-start(f32[1,64]{1,0:T(1,128)S(1)} %get-tuple-element.299), channel_id=1, source_target_pairs={{28,0},{0,4},{4,8},{8,12},{12,16},{16,20},{20,24},{24,28},{29,1},{... | collective-permute-start | bytes 776 | tf_op jit(solution)/shard_map/while/body/eval_jaxpr/ppermute | solution.py:19
  118.6 6.4 %collective-permute-start.2 = (f32[1,64]{1,0:T(1,128)S(1)}, f32[1,64]{1,0:T(1,128)S(1)}, u32[]{:S(2)}, u32[]{:S(2)}) collective-permute-start(f32[1,64]{1,0:T(1,128)S(1)} %get-tuple-element.300), channel_id=1, source_target_pairs={{28,0},{0,4},{4,8},{8,12},{12,16},{16,20},{20,24},{24,28},{29,1},{... | collective-permute-start | bytes 776 | tf_op jit(solution)/shard_map/while/body/eval_jaxpr/ppermute | solution.py:19
  132.8 7.0 %collective-permute-start.3 = (f32[1,64,512]{2,1,0:T(8,128)S(1)}, f32[1,64,512]{2,1,0:T(8,128)}, u32[]{:S(2)}, u32[]{:S(2)}) collective-permute-start(f32[1,64,512]{2,1,0:T(8,128)S(1)} %fusion.112), channel_id=1, source_target_pairs={{28,0},{0,4},{4,8},{8,12},{12,16},{16,20},{20,24},{24,28},{29,1},{... | collective-permute-start | bytes 393224 | tf_op jit(solution)/shard_map/while/body/eval_jaxpr/ppermute | solution.py:19
  132.9 6.9 %collective-permute-start = (bf16[1,36864]{1,0:T(2,128)(2,1)S(1)}, bf16[1,36864]{1,0:T(2,128)(2,1)S(1)}, u32[]{:S(2)}, u32[]{:S(2)}) collective-permute-start(bf16[1,36864]{1,0:T(2,128)(2,1)S(1)} %copy.27), channel_id=1, source_target_pairs={{28,0},{0,4},{4,8},{8,12},{12,16},{16,20},{20,24},{24,28},{29,1},{... | collective-permute-start | bytes 221192 | tf_op jit(solution)/shard_map/while/body/eval_jaxpr/ppermute | solution.py:19
  133.0 6.8 %collective-permute-start.1 = (f32[1,64]{1,0:T(1,128)S(1)}, f32[1,64]{1,0:T(1,128)S(1)}, u32[]{:S(2)}, u32[]{:S(2)}) collective-permute-start(f32[1,64]{1,0:T(1,128)S(1)} %get-tuple-element.299), channel_id=1, source_target_pairs={{28,0},{0,4},{4,8},{8,12},{12,16},{16,20},{20,24},{24,28},{29,1},{... | collective-permute-start | bytes 776 | tf_op jit(solution)/shard_map/while/body/eval_jaxpr/ppermute | solution.py:19
  133.4 6.4 %collective-permute-start.2 = (f32[1,64]{1,0:T(1,128)S(1)}, f32[1,64]{1,0:T(1,128)S(1)}, u32[]{:S(2)}, u32[]{:S(2)}) collective-permute-start(f32[1,64]{1,0:T(1,128)S(1)} %get-tuple-element.300), channel_id=1, source_target_pairs={{28,0},{0,4},{4,8},{8,12},{12,16},{16,20},{20,24},{24,28},{29,1},{... | collective-permute-start | bytes 776 | tf_op jit(solution)/shard_map/while/body/eval_jaxpr/ppermute | solution.py:19
  148.6 8.6 %all-to-all-start = ((bf16[8,1,8,512]{3,2,1,0:T(8,128)(2,1)}), bf16[8,1,8,512]{3,2,1,0:T(8,128)(2,1)S(1)}, u32[]{:S(2)}, u32[]{:S(2)}) async-start(bf16[8,1,8,512]{3,2,1,0:T(8,128)(2,1)} %constant_dynamic-update-slice_fusion), calls=%async_computation | async-start | bytes 131072 | tf_op jit(solution)/shard_map/all_to_all | solution.py:136
  152.1 66.0 %all-reduce.3.cloned.1.call-start = ((), (), s32[]{:S(2)}) async-start(), calls=%async_computation.1 | async-start | bytes 229376
  (16 other events, 366.2 us)
Sparse Core Ops, SparseCore 0:
  166.7 51.3 all-reduce.2
